TPU v7x, 32 devices: a whole 2x2x4 slice. The times are simulated.
32 devices in a mesh: ctx: 8 (over y, x, core), chan: 4 (over z).
Axes of the slice: x: 2, y: 2, z: 4, core: 2. Of those that a mesh axis runs over, the one named last changes fastest.
Arguments:
- queries: bfloat16 [1024, 4096], P('ctx', 'chan'), may hold values from -8 to 8
- key_rows: bfloat16 [1024, 4096], P('ctx', 'chan'), may hold values from -8 to 8
- value_rows: bfloat16 [1024, 4096], P('ctx', 'chan'), may hold values from -16 to 16
- gate_in: bfloat16 [1024, 4096], P('ctx', 'chan'), may hold values from -6 to 6
- gate_out: bfloat16 [1024, 4096], P('ctx', 'chan'), may hold values from -6 to 6
- kernel_taps: float32 [512, 7], P('chan'), may hold values from -2 to 2
- norm_gain: float32 [4096], P('chan'), may hold values from 0.1 to 1.9
- cotangent: bfloat16 [1024, 4096], P('ctx', 'chan'), may hold values from -6 to 6
Outputs:
- mixed: bfloat16 [1024, 4096], P('ctx', 'chan')
- grad_queries: bfloat16 [1024, 4096], P('ctx', 'chan')
- grad_keys: bfloat16 [1024, 4096], P('ctx', 'chan')
- grad_values: bfloat16 [1024, 4096], P('ctx', 'chan')
- grad_gate_in: bfloat16 [1024, 4096], P('ctx', 'chan')
- grad_gate_out: bfloat16 [1024, 4096], P('ctx', 'chan')
- grad_filter: float32 [512, 7], P('chan')
- grad_gain: float32 [4096], P('chan')
All inputs are finite; a program needn't handle non-finite values.
Results may differ from a plain program's by a relative error of at most 0.015.
Values may be sent and summed in bfloat16 or wider, within the bound.
No kernel may reach another device: no remote copies, remote signals or barrier semaphores. Data moves between devices by JAX's collectives and lax.ppermute only.
A program may use at most 128 MiB of HBM per device.

v0:
```python
import jax
import jax.numpy as jnp
from jax import lax
from jax.sharding import PartitionSpec as P

HEAD = 128
FILT = 7
WIDTH = 4096
EPS = 1e-06
NEG = -1e30


def from_behind(shard, axis, by):
    length = lax.axis_size(axis)
    pairs = [(i, i + by) for i in range(length) if 0 <= i + by < length]
    return lax.ppermute(shard, axis, pairs)


def score_block(query_heads, key_block, query_pos, key_pos):
    scores = jnp.einsum(
        "rhe,khe->hrk", query_heads, key_block, preferred_element_type=jnp.float32
    ) * HEAD ** (-0.5)
    allowed = query_pos[:, None] >= key_pos[None, :]
    return jnp.where(allowed[None], scores, NEG)


def row_totals(query_heads, query_pos, block_count, keys_heads, block_rows):
    row_count = query_heads.shape[0]
    head_count = query_heads.shape[1]

    def advance(block_index, running):
        row_max, row_sum = running
        first_key = block_index * block_rows
        key_block = lax.dynamic_slice_in_dim(keys_heads, first_key, block_rows, 0)
        key_pos = first_key + jnp.arange(block_rows, dtype=jnp.int32)
        scores = score_block(query_heads, key_block, query_pos, key_pos)
        new_max = jnp.maximum(row_max, jnp.max(scores, axis=2))
        row_sum = row_sum * jnp.exp(row_max - new_max) + jnp.sum(
            jnp.exp(scores - new_max[:, :, None]), axis=2
        )
        return (new_max, row_sum)

    initial = (
        jnp.full((head_count, row_count), NEG, jnp.float32),
        jnp.zeros((head_count, row_count), jnp.float32),
    )
    row_max, row_sum = lax.fori_loop(0, block_count, advance, initial)
    return row_max + jnp.log(row_sum)


def row_outputs(query_heads, query_pos, block_count, keys_heads, values_heads, lse, block_rows):
    row_count = query_heads.shape[0]
    head_count = query_heads.shape[1]

    def advance(block_index, summed):
        first_key = block_index * block_rows
        key_block = lax.dynamic_slice_in_dim(keys_heads, first_key, block_rows, 0)
        value_block = lax.dynamic_slice_in_dim(values_heads, first_key, block_rows, 0)
        key_pos = first_key + jnp.arange(block_rows, dtype=jnp.int32)
        scores = score_block(query_heads, key_block, query_pos, key_pos)
        weights_low = jnp.exp(scores - lse[:, :, None]).astype(jnp.bfloat16)
        return summed + jnp.einsum(
            "hrk,khe->rhe", weights_low, value_block, preferred_element_type=jnp.float32
        )

    summed = lax.fori_loop(
        0, block_count, advance, jnp.zeros((row_count, head_count, HEAD), jnp.float32)
    )
    return summed.reshape(row_count, head_count * HEAD).astype(jnp.bfloat16)


def query_grads(
    query_heads, d_heads, query_pos, block_count, keys_heads, values_heads, lse, delta, block_rows
):
    row_count = query_heads.shape[0]
    head_count = query_heads.shape[1]

    def advance(block_index, summed):
        first_key = block_index * block_rows
        key_block = lax.dynamic_slice_in_dim(keys_heads, first_key, block_rows, 0)
        value_block = lax.dynamic_slice_in_dim(values_heads, first_key, block_rows, 0)
        key_pos = first_key + jnp.arange(block_rows, dtype=jnp.int32)
        scores = score_block(query_heads, key_block, query_pos, key_pos)
        weights = jnp.exp(scores - lse[:, :, None])
        d_probs = jnp.einsum(
            "rhe,khe->hrk", d_heads, value_block, preferred_element_type=jnp.float32
        )
        d_scores = (weights * (d_probs - delta[:, :, None])).astype(jnp.bfloat16)
        return summed + jnp.einsum(
            "hrk,khe->rhe", d_scores, key_block, preferred_element_type=jnp.float32
        )

    summed = lax.fori_loop(
        0, block_count, advance, jnp.zeros((row_count, head_count, HEAD), jnp.float32)
    )
    return (summed * HEAD ** (-0.5)).reshape(row_count, head_count * HEAD).astype(jnp.bfloat16)


def shards(queries, key_rows, value_rows, gate_in, gate_out, kernel_taps, norm_gain, cotangent):
    row_count = queries.shape[0]
    channels = queries.shape[1]
    head_count = channels // HEAD
    group_count = kernel_taps.shape[0]
    devices = lax.axis_size("ctx")
    position = lax.axis_index("ctx")
    own_first = position * row_count
    total_rows = row_count * devices
    block_rows = min(512, total_rows)
    local_pos = jnp.arange(row_count, dtype=jnp.int32)
    keys_all, values_all = (
        lax.all_gather(key_rows, "ctx", axis=0, tiled=True),
        lax.all_gather(value_rows, "ctx", axis=0, tiled=True),
    )
    keys_heads = keys_all.reshape(total_rows, head_count, HEAD)
    query_sets = (queries, own_first + local_pos)
    query_block, query_pos = query_sets
    block_count = query_pos[-1] // block_rows + 1
    lse_sets = row_totals(
        query_block.reshape(-1, head_count, HEAD), query_pos, block_count, keys_heads, block_rows
    )
    values_heads = values_all.reshape(total_rows, head_count, HEAD)
    query_block, query_pos = query_sets
    outputs = row_outputs(
        query_block.reshape(-1, head_count, HEAD),
        query_pos,
        block_count,
        keys_heads,
        values_heads,
        lse_sets,
        block_rows,
    )
    lse_rows = lse_sets.T
    attn_wide = outputs.astype(jnp.float32)
    square_sum = lax.psum(jnp.sum(attn_wide * attn_wide, axis=1), "chan")
    inverse_rms = 1.0 / jnp.sqrt(square_sum / WIDTH + EPS)
    normed = attn_wide * inverse_rms[:, None] * norm_gain[None, :]
    gate_wide = gate_in.astype(jnp.float32)
    mixed_in = gate_wide * normed
    taps = jnp.broadcast_to(
        kernel_taps[:, None, :], (group_count, channels // group_count, FILT)
    ).reshape(channels, FILT)
    rim_before = from_behind(mixed_in[row_count - (FILT - 1) :], "ctx", 1)
    extended = jnp.concatenate([rim_before, mixed_in], axis=0)
    conv_out = jnp.zeros((row_count, channels), jnp.float32)
    for lag in range(FILT):
        conv_out = (
            conv_out + taps[:, lag][None, :] * extended[FILT - 1 - lag : FILT - 1 - lag + row_count]
        )
    out_gate = gate_out.astype(jnp.float32)
    mixed = (out_gate * conv_out).astype(jnp.bfloat16)
    upstream = cotangent.astype(jnp.float32)
    grad_gate_out = (upstream * conv_out).astype(jnp.bfloat16)
    d_conv = upstream * out_gate
    tap_columns = []
    for lag in range(FILT):
        per_channel = jnp.sum(
            d_conv * extended[FILT - 1 - lag : FILT - 1 - lag + row_count], axis=0
        )
        tap_columns.append(per_channel.reshape(group_count, -1).sum(axis=1))
    tap_terms = jnp.stack(tap_columns, axis=1)
    rim_after = from_behind(d_conv[: FILT - 1], "ctx", -1)
    extended_grad = jnp.concatenate([d_conv, rim_after], axis=0)
    d_mixed = jnp.zeros((row_count, channels), jnp.float32)
    for lag in range(FILT):
        d_mixed = d_mixed + taps[:, lag][None, :] * extended_grad[lag : lag + row_count]
    grad_gate_in = (d_mixed * normed).astype(jnp.bfloat16)
    d_normed = d_mixed * gate_wide
    gain_terms = jnp.sum(d_normed * attn_wide * inverse_rms[:, None], axis=0)
    grad_filter, grad_gain = lax.psum((tap_terms, gain_terms), "ctx")
    scaled = d_normed * norm_gain[None, :]
    row_dot = lax.psum(jnp.sum(scaled * attn_wide, axis=1), "chan")
    d_attn = (
        inverse_rms[:, None] * scaled - attn_wide * (inverse_rms**3 * row_dot / WIDTH)[:, None]
    ).astype(jnp.bfloat16)
    d_heads = d_attn.reshape(row_count, head_count, HEAD)
    delta_rows = jnp.sum(
        d_heads.astype(jnp.float32) * attn_wide.reshape(row_count, head_count, HEAD), axis=2
    )
    own_count = (own_first + row_count - 1) // block_rows + 1
    grad_queries = query_grads(
        queries.reshape(row_count, head_count, HEAD),
        d_heads,
        own_first + local_pos,
        own_count,
        keys_heads,
        values_heads,
        lse_rows.T,
        delta_rows.T,
        block_rows,
    )
    lse_all, delta_all = (
        lax.all_gather(lse_rows, "ctx", axis=0, tiled=True),
        lax.all_gather(delta_rows, "ctx", axis=0, tiled=True),
    )
    own_keys = key_rows.reshape(row_count, head_count, HEAD)
    own_values = value_rows.reshape(row_count, head_count, HEAD)
    key_pos = own_first + local_pos
    empty_grad = jnp.zeros((row_count, head_count, HEAD), jnp.float32)
    query_piece = lax.all_gather(queries, "ctx", axis=0, tiled=True)
    d_piece = lax.all_gather(d_attn, "ctx", axis=0, tiled=True)
    piece_rows = query_piece.shape[0]

    def contribute(totals):
        query_heads = query_piece.reshape(piece_rows, head_count, HEAD)
        piece_heads = d_piece.reshape(piece_rows, head_count, HEAD)
        query_pos = jnp.arange(piece_rows, dtype=jnp.int32)
        lse_piece = lse_all.T
        delta_piece = delta_all.T
        scores = score_block(query_heads, own_keys, query_pos, key_pos)
        weights = jnp.exp(scores - lse_piece[:, :, None])
        d_probs = jnp.einsum(
            "rhe,khe->hrk", piece_heads, own_values, preferred_element_type=jnp.float32
        )
        d_scores = (weights * (d_probs - delta_piece[:, :, None])).astype(jnp.bfloat16)
        key_grad = jnp.einsum(
            "hrk,rhe->khe", d_scores, query_heads, preferred_element_type=jnp.float32
        )
        value_grad = jnp.einsum(
            "hrk,rhe->khe",
            weights.astype(jnp.bfloat16),
            piece_heads,
            preferred_element_type=jnp.float32,
        )
        return (key_grad, value_grad)

    def unchanged(totals):
        return totals

    key_grad, value_grad = lax.cond(
        jnp.int32(0) + piece_rows > own_first, contribute, unchanged, (empty_grad, empty_grad)
    )
    grad_keys = (key_grad * HEAD ** (-0.5)).reshape(row_count, channels).astype(jnp.bfloat16)
    grad_values = value_grad.reshape(row_count, channels).astype(jnp.bfloat16)
    return (
        mixed,
        grad_queries,
        grad_keys,
        grad_values,
        grad_gate_in,
        grad_gate_out,
        grad_filter,
        grad_gain,
    )


def solution(mesh):
    placed = (
        P("ctx", "chan"),
        P("ctx", "chan"),
        P("ctx", "chan"),
        P("ctx", "chan"),
        P("ctx", "chan"),
        P("chan", None),
        P("chan"),
        P("ctx", "chan"),
    )
    return jax.shard_map(
        shards,
        mesh=mesh,
        in_specs=placed,
        out_specs=(
            P("ctx", "chan"),
            P("ctx", "chan"),
            P("ctx", "chan"),
            P("ctx", "chan"),
            P("ctx", "chan"),
            P("ctx", "chan"),
            P("chan", None),
            P("chan"),
        ),
        check_vma=False,
    )
```

profile of v0, /device:TPU:0, one launch (start us, length us, event | category | flops | bytes accessed | tf_op | source)
XLA Modules:
  0.0 189.7 jit_solution(9424736942254590684)
XLA Ops:
  7.2 1.8 copy.75
  9.1 1.8 copy.74
  11.0 1.1 convert_multiply_fusion.1
  12.1 0.8 copy-done.3
  12.9 1.3 collective-permute-start.1
  14.3 0.6 slice.80
  18.1 0.2 reshape.211
  18.3 23.0 %all-gather.7.cloned.1.call-done = bf16[1024,1024]{0,1:T(8,128)(2,1)} async-done(((bf16[128,1024]{0,1:T(8,128)(2,1)}), bf16[1024,1024]{0,1:T(8,128)(2,1)}) %all-gather.7.cloned.1.call-update) | async-done | bytes 2097168 | tf_op jit(solution)/shard_map/all_gather | solution.py:111
  41.3 3.0 %copy.79 = bf16[1024,8,128]{2,0,1:T(8,128)(2,1)S(1)} copy(bf16[1024,8,128]{0,2,1:T(8,128)(2,1)} %bitcast.151) | data formatting | bytes 4194304
  44.4 1.2 while.35
  44.6 0.5 fusion.130
  45.1 0.4 exponential_reduce_fusion.2
  45.6 26.3 %all-gather.5.cloned.1.call-done = bf16[1024,1024]{0,1:T(8,128)(2,1)} async-done(((bf16[128,1024]{0,1:T(8,128)(2,1)}), bf16[1024,1024]{0,1:T(8,128)(2,1)}) %all-gather.5.cloned.1.call-update) | async-done | bytes 2097168 | tf_op jit(solution)/shard_map/all_gather | solution.py:112
  71.9 2.4 %while.36 = (s32[]{:T(128)}, f32[128,8,128]{0,2,1:T(8,128)S(1)}, s32[]{:T(128)}, bf16[1024,8,128]{0,2,1:T(8,128)(2,1)}, bf16[1024,8,128]{2,0,1:T(8,128)(2,1)S(1)...) while((s32[]{:T(128)}, f32[128,8,128]{0,2,1:T(8,128)S(1)}, ...), condition=%wide.region_5.6_spmd.clone, body=%wide.region_4.5_spmd.clone.sunk | while | flops 270729856 | bytes 3549363 | solution.py:66
  72.1 2.2 %fusion.134 = f32[128,8,128]{0,2,1:T(8,128)S(1)} fusion(f32[128,8,128]{0,2,1:T(8,128)S(1)} %get-tuple-element.657, bf16[128,8,128]{2,0,1:T(8,128)(2,1)S(1)} %get-tuple-element.673, f32[8,128]{1,0:T(8,128)S(1)} %get-tuple-element.674, bf16[1024,8,128]{2,0,1:T(8,128)(2,1)S(1)} %get-tuple-element.672, s32[]{:T(128)S(6)} %select_n.93, ...), kind=kOutput, calls=%fused_computation.44.clone.1 | convolution fusion | flops 270663680 | bytes 3478528 | tf_op jit(solution)/shard_map/while/body/hrk,khe->rhe/dot_general | solution.py:62
  74.4 1.0 multiply_reduce_fusion.10
  75.3 11.7 %psum.28 = f32[128]{0:T(128)S(1)} all-reduce(f32[128]{0:T(128)S(1)} %get-tuple-element.441), channel_id=1, replica_groups=mesh['ctx'=8,'chan'=4] {'chan'}, use_global_device_ids=true, to_apply=%region_7.8 | all-reduce | flops 128 | bytes 1024 | tf_op jit(solution)/shard_map/psum | solution.py:134
  87.0 1.2 copy.97
  88.3 4.0 %multiply_convert_fusion.1 = (bf16[128,1024]{1,0:T(8,128)(2,1)}, f32[128,1024]{1,0:T(8,128)S(1)}) fusion(f32[128,1024]{1,0:T(8,128)S(1)} %copy.97, f32[1024]{0:T(1024)S(1)} %copy-done.10, f32[128]{0:T(128)S(1)} %add_rsqrt_fusion, f32[6,1024]{1,0:T(8,128)S(1)} %collective-permute-done.1, f32[128,1024]{1,0:T(8,128)} %copy-done.3, f32[1024]{0:T(1024)S(1)} %bitcast.162, ...), kind=kLoop, calls=%fused_computation.133 | loop fusion | flops 3014656 | bytes 1892864 | tf_op jit(solution)/shard_map/convert_element_type | solution.py:166
  92.3 0.8 copy-done.1
  93.1 0.2 multiply_reduce_fusion
  93.3 8.4 %psum.29 = f32[128]{0:T(128)S(1)} all-reduce(f32[128]{0:T(128)S(1)} %get-tuple-element.373), channel_id=1, replica_groups=mesh['ctx'=8,'chan'=4] {'chan'}, use_global_device_ids=true, to_apply=%region_9.10 | all-reduce | flops 128 | bytes 1024 | tf_op jit(solution)/shard_map/psum | solution.py:171
  101.7 2.0 %subtract_convert_fusion = (bf16[128,1024]{1,0:T(8,128)(2,1)}, f32[128,1024]{1,0:T(8,128)S(1)}) fusion(f32[128,1024]{1,0:T(8,128)S(1)} %copy.97, f32[128]{0:T(128)S(1)} %fusion.102, f32[1024]{0:T(1024)S(1)} %copy-done.10, f32[128]{0:T(128)S(1)} %add_rsqrt_fusion, f32[128,1024]{1,0:T(8,128)} %copy-done.1, bf16[128,1024]{1,0:T(8,128)(2,1)} %param.19), kind=kLoop, calls=%fused_computation.137 | loop fusion | flops 1310720 | bytes 2102272 | tf_op jit(solution)/shard_map/convert_element_type | solution.py:174
  103.8 0.6 slice.103
  104.4 1.3 collective-permute-start
  105.7 1.0 copy.109
  106.7 0.2 copy.82
  106.9 1.1 multiply_reduce_fusion.8
  108.0 1.0 copy_bitcast_fusion
  109.0 0.9 broadcast.128
  109.9 5.9 %while.37 = (s32[]{:T(128)}, f32[128,8,128]{0,2,1:T(8,128)}, s32[]{:T(128)}, bf16[1024,8,128]{2,0,1:T(8,128)(2,1)S(1)}, bf16[128,8,128]{2,0,1:T(8,128)(2,1)S(1)}...) while((s32[]{:T(128)}, f32[128,8,128]{0,2,1:T(8,128)}, ...), condition=%wide.region_12.13_spmd.clone, body=%wide.region_11.12_spmd.clone.sunk | while | flops 405996160 | bytes 9058503 | solution.py:93
  109.9 1.7 fusion.140
  111.8 4.1 %fusion.141 = f32[128,8,128]{0,2,1:T(8,128)} fusion(f32[128,8,128]{0,2,1:T(8,128)} %get-tuple-element.695, f32[8,512,128]{2,1,0:T(8,128)} %fusion.140, bf16[128,8,128]{2,0,1:T(8,128)(2,1)S(1)} %get-tuple-element.715, f32[8,128]{1,0:T(8,128)S(1)} %get-tuple-element.716, bf16[1024,8,128]{0,2,1:T(8,128)(2,1)} %get-tuple-element.714, s32[]{:T(128)S(6)} %select_n.95, ...), kind=kOutput, calls=%fused_computation.64.clone.1 | convolution fusion | flops 271712256 | bytes 5579776 | tf_op jit(solution)/shard_map/while/body/hrk,khe->rhe/dot_general | solution.py:89
  115.9 1.1 multiply_convert_fusion.3
  117.0 0.9 copy.98
  117.9 17.9 %all_gather.23 = f32[1024,8]{0,1:T(8,128)S(1)} all-gather(f32[128,8]{0,1:T(8,128)S(1)} %bitcast.178), channel_id=1, replica_groups=mesh['ctx'=8,'chan'=4] {'ctx'}, dimensions={0}, use_global_device_ids=true | all-gather | bytes 36864 | tf_op jit(solution)/shard_map/all_gather | solution.py:193
  135.8 8.5 %all_gather.21 = f32[1024,8]{0,1:T(8,128)S(1)} all-gather(f32[128,8]{0,1:T(8,128)S(1)} %bitcast.179), channel_id=1, replica_groups=mesh['ctx'=8,'chan'=4] {'ctx'}, dimensions={0}, use_global_device_ids=true | all-gather | bytes 36864 | tf_op jit(solution)/shard_map/all_gather | solution.py:192
  144.3 1.2 fusion.78
  145.5 1.2 multiply_reduce_fusion.1
  148.2 14.2 %all-reduce = (f32[128,7]{0,1:T(8,128)}, f32[1024]{0:T(1024)}) all-reduce(f32[128,7]{0,1:T(8,128)S(1)} %stack.31, f32[1024]{0:T(1024)S(1)} %get-tuple-element.372), channel_id=1, replica_groups=mesh['ctx'=8,'chan'=4] {'ctx'}, use_global_device_ids=true, to_apply=%region_29.30 | all-reduce | flops 1920 | bytes 15360 | tf_op jit(solution)/shard_map/psum | solution.py:169
  162.5 19.8 %conditional.1 = (f32[128,8,128]{0,2,1:T(8,128)S(1)}, bf16[128,1024]{1,0:T(8,128)(2,1)}) conditional(s32[]{:T(128)} %convert_element_type.91, () %tuple.33, (s32[128]{0:T(128)S(1)}, bf16[1024,1024]{1,0:T(8,128)(2,1)}, bf16[128,1024]{1,0:T(8,128)(2,1)S(1)}, f32[1024,8]{0,1:T(8,128)S(1)}, bf16[1024,1024]{1,0:T(8,128)(2,1)}, ...), branch_computations={%region_13.14_spmd, %region_14.15_spmd} | conditional | flops 1084489728 | bytes 38503096 | solution.py:229
  162.5 4.3 %fusion.11 = f32[8,1024,128]{2,1,0:T(8,128)} fusion(bf16[1024,1024]{1,0:T(8,128)(2,1)} %get-tuple-element.149, bf16[128,1024]{1,0:T(8,128)(2,1)S(1)} %get-tuple-element.150), kind=kOutput, calls=%fused_computation.9 | convolution fusion | flops 268435456 | bytes 6553600 | tf_op jit(solution)/shard_map/cond/branch_1_fun/rhe,khe->hrk/dot_general | solution.py:20
  166.8 4.1 %copy.88 = bf16[1024,1024]{0,1:T(8,128)(2,1)} copy(bf16[1024,1024]{1,0:T(8,128)(2,1)} %get-tuple-element.359) | data formatting | bytes 4194304 | tf_op jit(solution)/shard_map
  171.0 6.4 %fusion.19 = f32[128,8,128]{2,0,1:T(8,128)S(1)} fusion(f32[8,1024,128]{2,1,0:T(8,128)} %fusion.11, bf16[1024,8,128]{0,2,1:T(8,128)(2,1)} %bitcast.152, f32[8,1024]{1,0:T(8,128)S(1)} %bitcast.174, f32[8,1024]{1,0:T(8,128)S(1)} %bitcast.176, pred[1024,128]{1,0:T(8,128)(4,1)S(1)} %iota_compare_fusion, bf16[1024,1024]{1,0:T(8,128)(2,1)S(1)} %copy-done.4, ...), kind=kOutput, calls=%fused_computation.17 | convolution fusion | flops 543162368 | bytes 9371648 | tf_op jit(solution)/shard_map/cond/branch_1_fun/hrk,rhe->khe/dot_general | solution.py:215
  177.4 0.2 copy.101
  177.6 3.8 %fusion.22 = bf16[8,128,128]{1,2,0:T(8,128)(2,1)S(1)} fusion(bf16[1024,8,128]{0,2,1:T(8,128)(2,1)} %bitcast.153, f32[8,1024,128]{2,1,0:T(8,128)} %fusion.11, f32[8,1024]{1,0:T(8,128)} %bitcast.175, pred[1024,128]{1,0:T(8,128)(4,1)S(1)} %iota_compare_fusion), kind=kOutput, calls=%fused_computation.18 | convolution fusion | flops 272760832 | bytes 6717440 | tf_op jit(solution)/shard_map/cond/branch_1_fun/hrk,rhe->khe/dot_general | solution.py:218
  181.4 0.9 copy.103
  182.3 0.9 copy.99
  (83 shorter events, 2.9 us)
Async XLA Ops:
  7.2 9.7 %copy-start.6 = (bf16[128,1024]{1,0:T(8,128)(2,1)S(1)}, bf16[128,1024]{1,0:T(8,128)(2,1)}, u32[]{:S(2)}) copy-start(bf16[128,1024]{1,0:T(8,128)(2,1)} %param.16) | copy-start | bytes 786436
  7.2 10.7 %copy-start.15 = (f32[128,7]{0,1:T(8,128)S(1)}, f32[128,7]{0,1:T(8,128)}, u32[]{:S(2)}) copy-start(f32[128,7]{0,1:T(8,128)} %param.21) | copy-start | bytes 10756
  7.2 34.1 %all-gather.7.cloned.1.call-start = ((), (), s32[]{:S(2)}) async-start(), calls=%async_computation.1 | async-start | bytes 2359296 | tf_op jit(solution)/shard_map/all_gather | solution.py:111
  9.1 62.8 %all-gather.5.cloned.1.call-start = ((), (), s32[]{:S(2)}) async-start(), calls=%async_computation | async-start | bytes 2359296 | tf_op jit(solution)/shard_map/all_gather | solution.py:112
  10.9 151.5 %all-gather.9.cloned.1.call-start = ((), (), s32[]{:S(2)}) async-start(), calls=%async_computation.2 | async-start | bytes 2359296 | tf_op jit(solution)/shard_map/all_gather | solution.py:199
  12.1 0.8 copy-start.3
  12.9 75.4 %collective-permute-start.1 = (f32[6,1024]{1,0:T(8,128)S(1)}, f32[6,1024]{1,0:T(8,128)S(1)}, u32[]{:S(2)}, u32[]{:S(2)}) collective-permute-start(f32[6,1024]{1,0:T(8,128)S(1)} %slice.119), channel_id=1, source_target_pairs={{4,0},{8,4},{12,8},{16,12},{20,16},{24,20},{28,24},{5,1},{9,5},{13... | collective-permute-start | bytes 73736 | tf_op jit(solution)/shard_map/ppermute | solution.py:16
  14.2 148.2 %all-gather.11.cloned.1.call-start = ((), (), s32[]{:S(2)}) async-start(), calls=%async_computation.3 | async-start | bytes 2359296 | tf_op jit(solution)/shard_map/all_gather | solution.py:200
  74.3 19.0 %copy-start = (f32[128,8,128]{0,2,1:T(8,128)}, f32[128,8,128]{0,2,1:T(8,128)S(1)}, u32[]{:S(2)}) copy-start(f32[128,8,128]{0,2,1:T(8,128)S(1)} %get-tuple-element.171) | copy-start | bytes 1572868
  74.4 13.9 %copy-start.10 = (f32[1024]{0:T(1024)S(1)}, f32[1024]{0:T(1024)}, u32[]{:S(2)}) copy-start(f32[1024]{0:T(1024)} %param.22) | copy-start | bytes 12292
  88.3 4.9 %copy-start.7 = (bf16[128,1024]{1,0:T(8,128)(2,1)S(1)}, bf16[128,1024]{1,0:T(8,128)(2,1)}, u32[]{:S(2)}) copy-start(bf16[128,1024]{1,0:T(8,128)(2,1)} %param.19) | copy-start | bytes 786436
  92.3 0.8 copy-start.1
  104.4 39.9 %collective-permute-start = (f32[6,1024]{1,0:T(8,128)}, f32[6,1024]{1,0:T(8,128)S(1)}, u32[]{:S(2)}, u32[]{:S(2)}) collective-permute-start(f32[6,1024]{1,0:T(8,128)} %slice.103), channel_id=1, source_target_pairs={{0,4},{4,8},{8,12},{12,16},{16,20},{20,24},{24,28},{1,5},{5,9},{9,... | collective-permute-start | bytes 73736 | tf_op jit(solution)/shard_map/ppermute | solution.py:16
  109.9 34.4 %copy-start.2 = (bf16[128,1024]{1,0:T(8,128)(2,1)S(1)}, bf16[128,1024]{1,0:T(8,128)(2,1)}, u32[]{:S(2)}) copy-start(bf16[128,1024]{1,0:T(8,128)(2,1)} %param.23) | copy-start | bytes 786436
  115.9 29.6 %copy-start.8 = (bf16[128,1024]{1,0:T(8,128)(2,1)S(1)}, bf16[128,1024]{1,0:T(8,128)(2,1)}, u32[]{:S(2)}) copy-start(bf16[128,1024]{1,0:T(8,128)(2,1)} %param.20) | copy-start | bytes 786436
  144.3 18.1 %copy-start.5 = (bf16[128,1024]{1,0:T(8,128)(2,1)S(1)}, bf16[128,1024]{1,0:T(8,128)(2,1)}, u32[]{:S(2)}) copy-start(bf16[128,1024]{1,0:T(8,128)(2,1)} %param.17) | copy-start | bytes 786436
  162.5 4.3 %copy-start.11 = (f32[1024,8]{0,1:T(8,128)}, f32[1024,8]{0,1:T(8,128)S(1)}, u32[]{:S(2)}) copy-start(f32[1024,8]{0,1:T(8,128)S(1)} %get-tuple-element.154) | copy-start | bytes 98308 | tf_op jit(solution)/shard_map/cond
  162.5 4.3 %copy-start.13 = (f32[1024,8]{0,1:T(8,128)}, f32[1024,8]{0,1:T(8,128)S(1)}, u32[]{:S(2)}) copy-start(f32[1024,8]{0,1:T(8,128)S(1)} %get-tuple-element.151) | copy-start | bytes 98308 | tf_op jit(solution)/shard_map/cond
  166.7 4.2 %copy-start.4 = (bf16[1024,1024]{1,0:T(8,128)(2,1)S(1)}, bf16[1024,1024]{1,0:T(8,128)(2,1)}, u32[]{:S(2)}) copy-start(bf16[1024,1024]{1,0:T(8,128)(2,1)} %get-tuple-element.149) | copy-start | bytes 6291460 | tf_op jit(solution)/shard_map/cond
  166.7 4.2 %copy-start.9 = (bf16[128,1024]{1,0:T(8,128)(2,1)S(1)}, bf16[128,1024]{1,0:T(8,128)(2,1)}, u32[]{:S(2)}) copy-start(bf16[128,1024]{1,0:T(8,128)(2,1)} %get-tuple-element.153) | copy-start | bytes 786436 | tf_op jit(solution)/shard_map/cond
  166.7 4.2 %copy-start.12 = (f32[1024,8]{0,1:T(8,128)S(1)}, f32[1024,8]{0,1:T(8,128)}, u32[]{:S(2)}) copy-start(f32[1024,8]{0,1:T(8,128)} %copy-done.11) | copy-start | bytes 98308 | tf_op jit(solution)/shard_map/cond
  166.8 4.2 %copy-start.14 = (f32[1024,8]{0,1:T(8,128)S(1)}, f32[1024,8]{0,1:T(8,128)}, u32[]{:S(2)}) copy-start(f32[1024,8]{0,1:T(8,128)} %copy-done.13) | copy-start | bytes 98308 | tf_op jit(solution)/shard_map/cond
Sparse Core Ops, SparseCore 0:
  10.4 30.8 all-gather.6
  43.8 28.0 all-gather.4
  73.8 27.7 all-gather.8
  109.2 30.4 all-gather.10
where the time goes:
time: 190 us
  blocking collectives  60.7 us (32%)
  waiting for transfers between devices  49.4 us (26%)
  matrix products  22.9 us (12%)
  local copies, waits for them, and re-layouts  22.2 us (12%)
  between operations  16.7 us (9%)
  other arithmetic  14.8 us (8%)
  starting transfers between devices  2.72 us (1%)
    all_gather x1, waiting for transfers between devices, shards(): lax.all_gather(value_rows, 'ctx', axis=0, tiled=True)  26.3 us
    all_gather x1, waiting for transfers between devices, shards(): lax.all_gather(key_rows, 'ctx', axis=0, tiled=True)  23 us
    all_gather x1, blocking collectives, shards(): lax.all_gather(delta_rows, 'ctx', axis=0, tiled=True)  17.9 us
    psum x1, blocking collectives, shards(): grad_filter, grad_gain = lax.psum((tap_terms, gain_terms), 'ctx')  14.2 us
    psum x1, blocking collectives, shards(): square_sum = lax.psum(jnp.sum(attn_wide * attn_wide, axis=1), 'chan')  11.7 us
    unnamed x27, local copies, waits for them, and re-layouts  10.6 us
    all_gather x1, blocking collectives, shards(): lax.all_gather(lse_rows, 'ctx', axis=0, tiled=True)  8.53 us
    psum x1, blocking collectives, shards(): row_dot = lax.psum(jnp.sum(scaled * attn_wide, axis=1), 'chan')  8.37 us
  transfers between devices with their start and end apart: 6, of which 2 were waited for; matrix products, arithmetic and copies ran while one was open for 19% of the time, Pallas kernels for 0%

commit v1 on v0

--- a/solution.py
+++ b/solution.py
@@ -108,7 +108,9 @@
     block_rows = min(512, total_rows)
     local_pos = jnp.arange(row_count, dtype=jnp.int32)
     keys_all, values_all = (
-        lax.all_gather(key_rows, "ctx", axis=0, tiled=True),
+        jnp.concatenate(
+            lax.all_to_all(jnp.stack([key_rows] * lax.axis_size("ctx")), "ctx", 0, 0), axis=0
+        ),
         lax.all_gather(value_rows, "ctx", axis=0, tiled=True),
     )
     keys_heads = keys_all.reshape(total_rows, head_count, HEAD)

time: 190 us -> 174 us (0.916)
  waiting for transfers between devices: 49.4 us -> 28.7 us
  starting transfers between devices: 2.72 us -> 8.01 us
    all_to_all x0 -> x1, waiting for transfers between devices: none -> 28.7 us  [shards(): lax.all_to_all(jnp.stack([key_rows] * lax.axis_size('ctx')), 'ctx', 0, 0)]
    all_gather x1, waiting for transfers between devices: 26.3 us -> 0.01 us  [shards(): lax.all_gather(value_rows, 'ctx', axis=0, tiled=True)]
    all_gather x1 -> x0, waiting for transfers between devices: 23 us -> none  [shards(): lax.all_gather(key_rows, 'ctx', axis=0, tiled=True)]
    all_to_all x0 -> x1, starting transfers between devices: none -> 5.33 us  [shards(): lax.all_to_all(jnp.stack([key_rows] * lax.axis_size('ctx')), 'ctx', 0, 0)]
    unnamed x27 -> x31, local copies, waits for them, and re-layouts: 10.6 us -> 6.68 us
    another operation x3 -> x4, local copies, waits for them, and re-layouts: 5.01 us -> 7.52 us
  transfers between devices with their start and end apart: 6 -> 6, of which waited for: 2 -> 1; matrix products, arithmetic and copies ran while one was open for 19% -> 19% of each run, Pallas kernels for 0% -> 0%
where the time goes in v1:
time: 174 us; the launch traced here: 173 us
  blocking collectives  62.1 us (36%)
  waiting for transfers between devices  28.7 us (16%)
  matrix products  22.9 us (13%)
  local copies, waits for them, and re-layouts  20.7 us (12%)
  between operations  16.7 us (10%)
  other arithmetic  13.8 us (8%)
  starting transfers between devices  8.01 us (5%)
    all_to_all x1, waiting for transfers between devices, shards(): lax.all_to_all(jnp.stack([key_rows] * lax.axis_size('ctx')), 'ctx', 0, 0)  28.7 us
    all_gather x1, blocking collectives, shards(): lax.all_gather(delta_rows, 'ctx', axis=0, tiled=True)  17.4 us
    psum x1, blocking collectives, shards(): grad_filter, grad_gain = lax.psum((tap_terms, gain_terms), 'ctx')  14.1 us
    psum x1, blocking collectives, shards(): square_sum = lax.psum(jnp.sum(attn_wide * attn_wide, axis=1), 'chan')  11.9 us
    all_gather x1, blocking collectives, shards(): lax.all_gather(lse_rows, 'ctx', axis=0, tiled=True)  10.2 us
    psum x1, blocking collectives, shards(): row_dot = lax.psum(jnp.sum(scaled * attn_wide, axis=1), 'chan')  8.37 us
    unnamed x31, local copies, waits for them, and re-layouts  6.68 us
    dot_general x3, matrix products, score_block(): jnp.einsum('rhe,khe->hrk', query_heads, key_block, preferred_element_type...  6.43 us
  transfers between devices with their start and end apart: 6, of which 1 were waited for; matrix products, arithmetic and copies ran while one was open for 19% of the time, Pallas kernels for 0%

profile of v1, /device:TPU:0, one launch (start us, length us, event | category | flops | bytes accessed | tf_op | source)
XLA Modules:
  0.0 173.2 jit_solution(12265675006286035172)
XLA Ops:
  7.2 1.8 %copy.74 = bf16[128,1024]{0,1:T(8,128)(2,1)} copy(bf16[128,1024]{1,0:T(8,128)(2,1)} %param.18) | data formatting | bytes 524288 | tf_op args[2]
  9.0 2.5 %stack.35 = bf16[8,128,1024]{2,1,0:T(8,128)(2,1)} broadcast(bf16[128,1024]{1,0:T(8,128)(2,1)} %param.17), dimensions={1,2} | broadcast | bytes 2359296 | tf_op jit(solution)/shard_map/stack | solution.py:112
  11.5 5.3 %all-to-all-start = ((bf16[8,128,1024]{2,1,0:T(8,128)(2,1)}), bf16[8,128,1024]{2,1,0:T(8,128)(2,1)S(1)}, u32[]{:S(2)}, u32[]{:S(2)}) async-start(bf16[8,128,1024]{2,1,0:T(8,128)(2,1)} %stack.35), calls=%async_computation | async-start | bytes 4194304 | tf_op jit(solution)/shard_map/all_to_all | solution.py:112
  17.0 0.8 copy-done.4
  17.8 1.3 collective-permute-start.1
  19.2 0.6 slice.80
  23.0 0.2 reshape.210
  23.3 28.7 %all-to-all-done = bf16[8,128,1024]{2,1,0:T(8,128)(2,1)S(1)} async-done(((bf16[8,128,1024]{2,1,0:T(8,128)(2,1)}), bf16[8,128,1024]{2,1,0:T(8,128)(2,1)S(1)}, u32[]{:S(2)}, u32[]{:S(2)}) %all-to-all-start) | async-done | bytes 2097184 | tf_op jit(solution)/shard_map/all_to_all | solution.py:112
  51.9 0.6 copy.108
  52.5 0.3 copy.78
  52.8 1.2 while.35
  53.0 0.5 fusion.130
  53.5 0.4 exponential_reduce_fusion.2
  54.0 10.2 %all_gather.17 = f32[1024,8]{0,1:T(8,128)} all-gather(f32[128,8]{0,1:T(8,128)S(1)} %bitcast.182), channel_id=1, replica_groups=mesh['ctx'=8,'chan'=4] {'ctx'}, dimensions={0}, use_global_device_ids=true | all-gather | bytes 36864 | tf_op jit(solution)/shard_map/all_gather | solution.py:194
  64.3 2.4 %while.36 = (s32[]{:T(128)}, f32[128,8,128]{0,2,1:T(8,128)S(1)}, s32[]{:T(128)}, bf16[1024,8,128]{0,2,1:T(8,128)(2,1)}, bf16[1024,8,128]{2,0,1:T(8,128)(2,1)S(1)...) while((s32[]{:T(128)}, f32[128,8,128]{0,2,1:T(8,128)S(1)}, ...), condition=%wide.region_5.6_spmd.clone, body=%wide.region_4.5_spmd.clone.sunk | while | flops 270729856 | bytes 3549363 | solution.py:66
  64.5 2.2 %fusion.134 = f32[128,8,128]{0,2,1:T(8,128)S(1)} fusion(f32[128,8,128]{0,2,1:T(8,128)S(1)} %get-tuple-element.657, bf16[128,8,128]{2,0,1:T(8,128)(2,1)S(1)} %get-tuple-element.673, f32[8,128]{1,0:T(8,128)S(1)} %get-tuple-element.674, bf16[1024,8,128]{2,0,1:T(8,128)(2,1)S(1)} %get-tuple-element.672, s32[]{:T(128)S(6)} %select_n.93, ...), kind=kOutput, calls=%fused_computation.44.clone.1 | convolution fusion | flops 270663680 | bytes 3478528 | tf_op jit(solution)/shard_map/while/body/hrk,khe->rhe/dot_general | solution.py:62
  66.7 1.0 multiply_reduce_fusion.10
  67.7 11.9 %psum.28 = f32[128]{0:T(128)S(1)} all-reduce(f32[128]{0:T(128)S(1)} %get-tuple-element.441), channel_id=1, replica_groups=mesh['ctx'=8,'chan'=4] {'chan'}, use_global_device_ids=true, to_apply=%region_7.8 | all-reduce | flops 128 | bytes 1024 | tf_op jit(solution)/shard_map/psum | solution.py:136
  79.6 1.2 copy.96
  80.9 4.0 %multiply_convert_fusion.1 = (bf16[128,1024]{1,0:T(8,128)(2,1)}, f32[128,1024]{1,0:T(8,128)S(1)}) fusion(f32[128,1024]{1,0:T(8,128)S(1)} %copy.96, f32[1024]{0:T(1024)S(1)} %copy-done.12, f32[128]{0:T(128)S(1)} %add_rsqrt_fusion, f32[6,1024]{1,0:T(8,128)S(1)} %collective-permute-done.1, f32[128,1024]{1,0:T(8,128)} %copy-done.4, f32[1024]{0:T(1024)S(1)} %bitcast.165, ...), kind=kLoop, calls=%fused_computation.133 | loop fusion | flops 3014656 | bytes 1892864 | tf_op jit(solution)/shard_map/convert_element_type | solution.py:168
  84.9 0.8 copy-done.1
  85.7 0.2 multiply_reduce_fusion
  86.0 8.4 %psum.29 = f32[128]{0:T(128)S(1)} all-reduce(f32[128]{0:T(128)S(1)} %get-tuple-element.373), channel_id=1, replica_groups=mesh['ctx'=8,'chan'=4] {'chan'}, use_global_device_ids=true, to_apply=%region_9.10 | all-reduce | flops 128 | bytes 1024 | tf_op jit(solution)/shard_map/psum | solution.py:173
  94.4 2.0 %subtract_convert_fusion = (bf16[128,1024]{1,0:T(8,128)(2,1)}, f32[128,1024]{1,0:T(8,128)S(1)}) fusion(f32[128,1024]{1,0:T(8,128)S(1)} %copy.96, f32[128]{0:T(128)S(1)} %fusion.102, f32[1024]{0:T(1024)S(1)} %copy-done.12, f32[128]{0:T(128)S(1)} %add_rsqrt_fusion, f32[128,1024]{1,0:T(8,128)} %copy-done.1, bf16[128,1024]{1,0:T(8,128)(2,1)} %param.19), kind=kLoop, calls=%fused_computation.137 | loop fusion | flops 1310720 | bytes 2102272 | tf_op jit(solution)/shard_map/convert_element_type | solution.py:176
  96.4 0.6 slice.103
  97.0 1.3 collective-permute-start
  98.3 1.0 copy.109
  99.3 0.2 copy.81
  99.5 1.1 multiply_reduce_fusion.8
  100.6 1.0 copy_bitcast_fusion
  101.7 0.9 broadcast.130
  102.6 5.9 %while.37 = (s32[]{:T(128)}, f32[128,8,128]{0,2,1:T(8,128)}, s32[]{:T(128)}, bf16[1024,8,128]{2,0,1:T(8,128)(2,1)S(1)}, bf16[128,8,128]{2,0,1:T(8,128)(2,1)S(1)}...) while((s32[]{:T(128)}, f32[128,8,128]{0,2,1:T(8,128)}, ...), condition=%wide.region_12.13_spmd.clone, body=%wide.region_11.12_spmd.clone.sunk | while | flops 405996160 | bytes 9058503 | solution.py:93
  102.6 1.7 fusion.140
  104.4 4.1 %fusion.141 = f32[128,8,128]{0,2,1:T(8,128)} fusion(f32[128,8,128]{0,2,1:T(8,128)} %get-tuple-element.695, f32[8,512,128]{2,1,0:T(8,128)} %fusion.140, bf16[128,8,128]{2,0,1:T(8,128)(2,1)S(1)} %get-tuple-element.715, f32[8,128]{1,0:T(8,128)S(1)} %get-tuple-element.716, bf16[1024,8,128]{0,2,1:T(8,128)(2,1)} %get-tuple-element.714, s32[]{:T(128)S(6)} %select_n.95, ...), kind=kOutput, calls=%fused_computation.64.clone.1 | convolution fusion | flops 271712256 | bytes 5579776 | tf_op jit(solution)/shard_map/while/body/hrk,khe->rhe/dot_general | solution.py:89
  108.5 1.1 multiply_convert_fusion.3
  109.7 0.8 copy.97
  110.5 17.4 %all_gather.19 = f32[1024,8]{0,1:T(8,128)S(1)} all-gather(f32[128,8]{0,1:T(8,128)S(1)} %bitcast.181), channel_id=1, replica_groups=mesh['ctx'=8,'chan'=4] {'ctx'}, dimensions={0}, use_global_device_ids=true | all-gather | bytes 36864 | tf_op jit(solution)/shard_map/all_gather | solution.py:195
  128.0 1.2 fusion.78
  129.2 1.2 multiply_reduce_fusion.1
  131.9 14.1 %all-reduce = (f32[128,7]{0,1:T(8,128)}, f32[1024]{0:T(1024)}) all-reduce(f32[128,7]{0,1:T(8,128)S(1)} %stack.43, f32[1024]{0:T(1024)S(1)} %get-tuple-element.372), channel_id=1, replica_groups=mesh['ctx'=8,'chan'=4] {'ctx'}, use_global_device_ids=true, to_apply=%region_29.30 | all-reduce | flops 1920 | bytes 15360 | tf_op jit(solution)/shard_map/psum | solution.py:171
  146.0 19.8 %conditional.1 = (f32[128,8,128]{0,2,1:T(8,128)S(1)}, bf16[128,1024]{1,0:T(8,128)(2,1)}) conditional(s32[]{:T(128)} %convert_element_type.91, () %tuple.33, (s32[128]{0:T(128)S(1)}, bf16[1024,1024]{1,0:T(8,128)(2,1)}, bf16[128,1024]{1,0:T(8,128)(2,1)S(1)}, f32[1024,8]{0,1:T(8,128)}, bf16[1024,1024]{1,0:T(8,128)(2,1)}, ...), branch_computations={%region_13.14_spmd, %region_14.15_spmd} | conditional | flops 1084489728 | bytes 38371996 | solution.py:231
  146.0 4.2 %fusion.11 = f32[8,1024,128]{2,1,0:T(8,128)} fusion(bf16[1024,1024]{1,0:T(8,128)(2,1)} %get-tuple-element.149, bf16[128,1024]{1,0:T(8,128)(2,1)S(1)} %get-tuple-element.150), kind=kOutput, calls=%fused_computation.9 | convolution fusion | flops 268435456 | bytes 6553600 | tf_op jit(solution)/shard_map/cond/branch_1_fun/rhe,khe->hrk/dot_general | solution.py:20
  150.3 4.1 %copy.87 = bf16[1024,1024]{0,1:T(8,128)(2,1)} copy(bf16[1024,1024]{1,0:T(8,128)(2,1)} %get-tuple-element.359) | data formatting | bytes 4194304 | tf_op jit(solution)/shard_map
  154.5 6.4 %fusion.19 = f32[128,8,128]{2,0,1:T(8,128)S(1)} fusion(f32[8,1024,128]{2,1,0:T(8,128)} %fusion.11, bf16[1024,8,128]{0,2,1:T(8,128)(2,1)} %bitcast.155, f32[8,1024]{1,0:T(8,128)S(1)} %bitcast.179, f32[8,1024]{1,0:T(8,128)S(1)} %bitcast.178, pred[1024,128]{1,0:T(8,128)(4,1)S(1)} %iota_compare_fusion, bf16[1024,1024]{1,0:T(8,128)(2,1)S(1)} %copy-done.5, ...), kind=kOutput, calls=%fused_computation.17 | convolution fusion | flops 543162368 | bytes 9371648 | tf_op jit(solution)/shard_map/cond/branch_1_fun/hrk,rhe->khe/dot_general | solution.py:217
  160.9 0.2 copy.100
  161.1 3.8 %fusion.22 = bf16[8,128,128]{1,2,0:T(8,128)(2,1)S(1)} fusion(bf16[1024,8,128]{0,2,1:T(8,128)(2,1)} %bitcast.156, f32[8,1024,128]{2,1,0:T(8,128)} %fusion.11, f32[8,1024]{1,0:T(8,128)} %bitcast.177, pred[1024,128]{1,0:T(8,128)(4,1)S(1)} %iota_compare_fusion), kind=kOutput, calls=%fused_computation.18 | convolution fusion | flops 272760832 | bytes 6717440 | tf_op jit(solution)/shard_map/cond/branch_1_fun/hrk,rhe->khe/dot_general | solution.py:220
  164.9 0.8 copy.102
  165.8 0.8 copy.98
  (85 shorter events, 2.9 us)
Async XLA Ops:
  7.2 57.1 %all-gather.4.cloned.1.call-start = ((), (), s32[]{:S(2)}) async-start(), calls=%async_computation.1 | async-start | bytes 2359296 | tf_op jit(solution)/shard_map/all_gather | solution.py:114
  11.5 5.4 %copy-start.2 = (bf16[128,1024]{1,0:T(8,128)(2,1)S(1)}, bf16[128,1024]{1,0:T(8,128)(2,1)}, u32[]{:S(2)}) copy-start(bf16[128,1024]{1,0:T(8,128)(2,1)} %param.23) | copy-start | bytes 786436
  11.5 5.4 %copy-start.9 = (bf16[128,1024]{1,0:T(8,128)(2,1)S(1)}, bf16[128,1024]{1,0:T(8,128)(2,1)}, u32[]{:S(2)}) copy-start(bf16[128,1024]{1,0:T(8,128)(2,1)} %param.20) | copy-start | bytes 786436
  11.5 10.2 %copy-start.7 = (bf16[128,1024]{1,0:T(8,128)(2,1)S(1)}, bf16[128,1024]{1,0:T(8,128)(2,1)}, u32[]{:S(2)}) copy-start(bf16[128,1024]{1,0:T(8,128)(2,1)} %param.16) | copy-start | bytes 786436
  11.5 40.4 %all-to-all-start = ((bf16[8,128,1024]{2,1,0:T(8,128)(2,1)}), bf16[8,128,1024]{2,1,0:T(8,128)(2,1)S(1)}, u32[]{:S(2)}, u32[]{:S(2)}) async-start(bf16[8,128,1024]{2,1,0:T(8,128)(2,1)} %stack.35), calls=%async_computation | async-start | bytes 4194304 | tf_op jit(solution)/shard_map/all_to_all | solution.py:112
  16.9 5.9 %copy-start.16 = (f32[128,7]{0,1:T(8,128)S(1)}, f32[128,7]{0,1:T(8,128)}, u32[]{:S(2)}) copy-start(f32[128,7]{0,1:T(8,128)} %param.21) | copy-start | bytes 10756
  16.9 129.1 %all-gather.6.cloned.1.call-start = ((), (), s32[]{:S(2)}) async-start(), calls=%async_computation.2 | async-start | bytes 2359296 | tf_op jit(solution)/shard_map/all_gather | solution.py:201
  17.0 0.8 copy-start.4
  17.8 63.1 %collective-permute-start.1 = (f32[6,1024]{1,0:T(8,128)S(1)}, f32[6,1024]{1,0:T(8,128)S(1)}, u32[]{:S(2)}, u32[]{:S(2)}) collective-permute-start(f32[6,1024]{1,0:T(8,128)S(1)} %slice.119), channel_id=1, source_target_pairs={{4,0},{8,4},{12,8},{16,12},{20,16},{24,20},{28,24},{5,1},{9,5},{13... | collective-permute-start | bytes 73736 | tf_op jit(solution)/shard_map/ppermute | solution.py:16
  19.1 126.9 %all-gather.8.cloned.1.call-start = ((), (), s32[]{:S(2)}) async-start(), calls=%async_computation.3 | async-start | bytes 2359296 | tf_op jit(solution)/shard_map/all_gather | solution.py:202
  66.7 19.3 %copy-start = (f32[128,8,128]{0,2,1:T(8,128)}, f32[128,8,128]{0,2,1:T(8,128)S(1)}, u32[]{:S(2)}) copy-start(f32[128,8,128]{0,2,1:T(8,128)S(1)} %get-tuple-element.171) | copy-start | bytes 1572868
  66.7 14.2 %copy-start.12 = (f32[1024]{0:T(1024)S(1)}, f32[1024]{0:T(1024)}, u32[]{:S(2)}) copy-start(f32[1024]{0:T(1024)} %param.22) | copy-start | bytes 12292
  80.9 4.9 %copy-start.8 = (bf16[128,1024]{1,0:T(8,128)(2,1)S(1)}, bf16[128,1024]{1,0:T(8,128)(2,1)}, u32[]{:S(2)}) copy-start(bf16[128,1024]{1,0:T(8,128)(2,1)} %param.19) | copy-start | bytes 786436
  84.9 0.8 copy-start.1
  97.0 31.0 %collective-permute-start = (f32[6,1024]{1,0:T(8,128)}, f32[6,1024]{1,0:T(8,128)S(1)}, u32[]{:S(2)}, u32[]{:S(2)}) collective-permute-start(f32[6,1024]{1,0:T(8,128)} %slice.103), channel_id=1, source_target_pairs={{0,4},{4,8},{8,12},{12,16},{16,20},{20,24},{24,28},{1,5},{5,9},{9,... | collective-permute-start | bytes 73736 | tf_op jit(solution)/shard_map/ppermute | solution.py:16
  102.6 25.4 %copy-start.3 = (bf16[128,1024]{1,0:T(8,128)(2,1)S(1)}, bf16[128,1024]{1,0:T(8,128)(2,1)}, u32[]{:S(2)}) copy-start(bf16[128,1024]{1,0:T(8,128)(2,1)} %param.23) | copy-start | bytes 786436
  108.5 20.7 %copy-start.10 = (bf16[128,1024]{1,0:T(8,128)(2,1)S(1)}, bf16[128,1024]{1,0:T(8,128)(2,1)}, u32[]{:S(2)}) copy-start(bf16[128,1024]{1,0:T(8,128)(2,1)} %param.20) | copy-start | bytes 786436
  128.0 18.1 %copy-start.6 = (bf16[128,1024]{1,0:T(8,128)(2,1)S(1)}, bf16[128,1024]{1,0:T(8,128)(2,1)}, u32[]{:S(2)}) copy-start(bf16[128,1024]{1,0:T(8,128)(2,1)} %param.17) | copy-start | bytes 786436
  146.0 4.2 %copy-start.14 = (f32[1024,8]{0,1:T(8,128)}, f32[1024,8]{0,1:T(8,128)S(1)}, u32[]{:S(2)}) copy-start(f32[1024,8]{0,1:T(8,128)S(1)} %get-tuple-element.154) | copy-start | bytes 98308 | tf_op jit(solution)/shard_map/cond
  150.3 4.2 %copy-start.5 = (bf16[1024,1024]{1,0:T(8,128)(2,1)S(1)}, bf16[1024,1024]{1,0:T(8,128)(2,1)}, u32[]{:S(2)}) copy-start(bf16[1024,1024]{1,0:T(8,128)(2,1)} %get-tuple-element.149) | copy-start | bytes 6291460 | tf_op jit(solution)/shard_map/cond
  150.3 4.2 %copy-start.11 = (bf16[128,1024]{1,0:T(8,128)(2,1)S(1)}, bf16[128,1024]{1,0:T(8,128)(2,1)}, u32[]{:S(2)}) copy-start(bf16[128,1024]{1,0:T(8,128)(2,1)} %get-tuple-element.153) | copy-start | bytes 786436 | tf_op jit(solution)/shard_map/cond
  150.3 4.2 %copy-start.13 = (f32[1024,8]{0,1:T(8,128)S(1)}, f32[1024,8]{0,1:T(8,128)}, u32[]{:S(2)}) copy-start(f32[1024,8]{0,1:T(8,128)} %get-tuple-element.151) | copy-start | bytes 98308 | tf_op jit(solution)/shard_map/cond
  150.3 4.2 %copy-start.15 = (f32[1024,8]{0,1:T(8,128)S(1)}, f32[1024,8]{0,1:T(8,128)}, u32[]{:S(2)}) copy-start(f32[1024,8]{0,1:T(8,128)} %copy-done.14) | copy-start | bytes 98308 | tf_op jit(solution)/shard_map/cond
Sparse Core Ops, SparseCore 0:
  10.4 41.6 all-gather.3
  54.0 28.8 all-gather.5
  101.8 29.9 all-gather.7
